TPU v7x, 32 devices: a whole 2x2x4 slice. The times are simulated.
32 devices in a mesh: gy: 4 (over x, core), gx: 4 (over z), probe: 2 (over y).
Axes of the slice: x: 2, y: 2, z: 4, core: 2. Of those that a mesh axis runs over, the one named last changes fastest.
Arguments:
- state: bfloat16 [4, 16, 16, 640], P(None, 'gy', 'gx'), may hold values from -6 to 6
- probe_signs: int32 [4, 4, 16, 16, 640], P('probe', None, 'gy', 'gx'), may hold values from -1 to 1, as said below
- timesteps: int32 [4], replicated, may hold values from 0 to 999
- time_table: float32 [1000, 640], replicated, may hold values from -4 to 4
- gn_gain: float32 [640], replicated, may hold values from 0.5 to 1.5
- gn_shift: float32 [640], replicated, may hold values from -3 to 3
- conv_weight: bfloat16 [9, 640, 640], P(None, 'probe'), may hold values from -0.078125 to 0.078125
- conv_bias: float32 [640], replicated, may hold values from -3 to 3
Outputs:
- next_state: bfloat16 [4, 16, 16, 640], P(None, 'gy', 'gx')
- logp_delta: float32 [4], replicated
Inputs may be any that keep to these rules, and one draw needn't show every extreme that they name: `probe_signs`: every entry is -1 or 1.
All inputs are finite; a program needn't handle non-finite values.
Results may differ from a plain program's by a relative error of at most 0.0034.
Values may be sent and summed in bfloat16 or wider, within the bound.
A program may use at most 64 MiB of HBM per device.

v0:
```python
import jax
import jax.numpy as jnp
from jax import lax
from jax.sharding import PartitionSpec as P

GROUPS = 32


def with_halo(block, sides, width):
    for axis, dim in sides:
        count = lax.axis_size(axis)
        forward = [(i, i + 1) for i in range(count - 1)]
        backward = [(target, source) for source, target in forward]
        low = lax.ppermute(
            lax.slice_in_dim(block, block.shape[dim] - width, None, axis=dim), axis, forward
        )
        high = lax.ppermute(lax.slice_in_dim(block, 0, width, axis=dim), axis, backward)
        block = jnp.concatenate([low, block, high], axis=dim)
    return block


def local_conv(padded, weight, height, width):
    count = padded.shape[0]
    chans = padded.shape[3]
    total = jnp.zeros((count * height * width, weight.shape[2]), jnp.float32)
    for tap in range(9):
        row_off = tap // 3
        col_off = tap % 3
        window = padded[:, row_off : row_off + height, col_off : col_off + width, :].reshape(
            -1, chans
        )
        total = total + jnp.dot(window, weight[tap], preferred_element_type=jnp.float32)
    return total


def travelling_probes(
    state, probe_signs, timesteps, time_table, gn_gain, gn_shift, conv_weight, conv_bias
):
    batch, tile_h, tile_w, chans = state.shape
    share = conv_weight.shape[1]
    group_width = chans // GROUPS
    ny, nx = (lax.axis_size("gy"), lax.axis_size("gx"))
    count = tile_h * ny * tile_w * nx * group_width
    xf = state.astype(jnp.float32)
    signs = lax.all_gather(probe_signs.astype(jnp.bfloat16), "probe", axis=0, tiled=True)
    probes = signs.shape[0]
    first = lax.axis_index("probe") * share

    def mine(array):
        return lax.dynamic_slice_in_dim(array, first, share, axis=array.ndim - 1)

    stacked = jnp.concatenate([state[None], signs], axis=0)
    stacked = mine(stacked).reshape((1 + probes) * batch, tile_h, tile_w, share)
    padded = with_halo(stacked, (("gy", 1), ("gx", 2)), 1)
    padded = padded.reshape(1 + probes, batch, tile_h + 2, tile_w + 2, share).astype(jnp.float32)
    cells_x = jnp.stack([jnp.sum(xf, axis=(1, 2)), jnp.sum(xf * xf, axis=(1, 2))])
    signs_f = signs.astype(jnp.float32)
    cells_u = jnp.stack([jnp.sum(signs_f, axis=(2, 3)), jnp.sum(signs_f * xf[None], axis=(2, 3))])
    cells = jnp.concatenate([cells_x, cells_u.reshape(2 * probes, batch, chans)], axis=0)
    sums = jnp.sum(cells.reshape(2 + 2 * probes, batch, GROUPS, group_width), axis=3)
    sums = lax.psum(sums, ("gy", "gx")) / count
    mean_x, mean_xx = (sums[0], sums[1])
    mean_u, cross = (sums[2 : 2 + probes], sums[2 + probes :])
    sigma = jnp.sqrt(mean_xx - mean_x * mean_x + 1e-05)
    mean_cu = cross - mean_x[None] * mean_u
    inv = 1.0 / sigma
    table = jnp.concatenate([mean_x[None], inv[None], mean_u, mean_cu * (inv * inv * inv)], axis=0)
    table = mine(jnp.repeat(table, group_width, axis=2))[:, :, None, None, :]
    onehot = (
        timesteps[:, None] == jnp.arange(time_table.shape[0], dtype=jnp.int32)[None, :]
    ).astype(jnp.float32)
    embed = jnp.dot(onehot, time_table, precision=lax.Precision.HIGHEST)
    offset = mine(gn_shift + embed)[:, None, None, :]
    gain = mine(gn_gain)
    centered = padded[0] - table[0]
    pre = centered * table[1] * gain + offset
    sig = jax.nn.sigmoid(pre)
    rows = lax.axis_index("gy") * tile_h - 1 + jnp.arange(tile_h + 2)
    cols = lax.axis_index("gx") * tile_w - 1 + jnp.arange(tile_w + 2)
    inside = ((rows >= 0) & (rows < tile_h * ny))[:, None] & ((cols >= 0) & (cols < tile_w * nx))[
        None, :
    ]
    inside = inside[:, :, None]
    hidden = jnp.where(inside, pre * sig, 0.0).astype(jnp.bfloat16)
    slope = jnp.where(inside, sig * (1.0 + pre * (1.0 - sig)) * gain, 0.0)
    dnormal = (padded[1:] - table[2 : 2 + probes]) * table[1] - centered * table[2 + probes :]
    dhidden = (slope[None] * dnormal).astype(jnp.bfloat16)
    velocity = local_conv(hidden, conv_weight, tile_h, tile_w)
    velocity = lax.psum(velocity, "probe").reshape(batch, tile_h, tile_w, chans) + conv_bias
    next_state = (xf + 0.25 * velocity).astype(jnp.bfloat16)
    tangent = local_conv(
        dhidden.reshape(probes * batch, tile_h + 2, tile_w + 2, share), conv_weight, tile_h, tile_w
    ).reshape(signs.shape)
    total = lax.psum(jnp.sum(signs_f * tangent, axis=(0, 2, 3, 4)), ("gy", "gx", "probe"))
    return (next_state, -0.25 / probes * total)


def gathered_weights(
    state, probe_signs, timesteps, time_table, gn_gain, gn_shift, conv_weight, conv_bias
):
    batch, tile_h, tile_w, chans = state.shape
    probes_here = probe_signs.shape[0]
    group_width = chans // GROUPS
    count = tile_h * lax.axis_size("gy") * tile_w * lax.axis_size("gx") * group_width
    xf = state.astype(jnp.float32)
    signs = probe_signs.astype(jnp.float32)
    grouped = xf.reshape(batch, tile_h, tile_w, GROUPS, group_width)
    signs_grouped = signs.reshape(probes_here, batch, tile_h, tile_w, GROUPS, group_width)
    sum_x = jnp.sum(grouped, axis=(1, 2, 4))
    sum_xx = jnp.sum(grouped * grouped, axis=(1, 2, 4))
    sum_u = jnp.sum(signs_grouped, axis=(2, 3, 5))
    cross = jnp.sum(signs_grouped * grouped[None], axis=(2, 3, 5))
    sum_x, sum_xx, sum_u, cross = lax.psum((sum_x, sum_xx, sum_u, cross), ("gy", "gx"))
    mean_x = sum_x / count
    centered = grouped - mean_x[:, None, None, :, None]
    sum_cu = cross - mean_x[None] * sum_u
    var_x = sum_xx / count - mean_x * mean_x
    sigma = jnp.sqrt(var_x + 1e-05)[:, None, None, :, None]
    normal = (centered / sigma).reshape(batch, tile_h, tile_w, chans)
    mean_u = (sum_u / count)[:, :, None, None, :, None]
    mean_cu = (sum_cu / count)[:, :, None, None, :, None]
    dnormal = (signs_grouped - mean_u) / sigma[None] - centered[None] * mean_cu / (
        sigma * sigma * sigma
    )[None]
    dnormal = dnormal.reshape(probes_here, batch, tile_h, tile_w, chans)
    onehot = (
        timesteps[:, None] == jnp.arange(time_table.shape[0], dtype=jnp.int32)[None, :]
    ).astype(jnp.float32)
    embed = jnp.dot(onehot, time_table, precision=lax.Precision.HIGHEST)
    pre = normal * gn_gain + gn_shift + embed[:, None, None, :]
    sig = jax.nn.sigmoid(pre)
    hidden = (pre * sig).astype(jnp.bfloat16)
    slope = sig * (1.0 + pre * (1.0 - sig)) * gn_gain
    dhidden = (slope[None] * dnormal).astype(jnp.bfloat16)
    flat_tangents = dhidden.reshape(probes_here * batch, tile_h, tile_w, chans)
    stacked = jnp.concatenate([hidden, flat_tangents], axis=0)
    items = stacked.shape[0]
    padded = with_halo(stacked, (("gy", 1), ("gx", 2)), 1)
    summed = local_conv(
        padded, lax.all_gather(conv_weight, "probe", axis=1, tiled=True), tile_h, tile_w
    )
    conv_out = summed.reshape(items, tile_h, tile_w, chans)
    conv_primal = conv_out[:batch]
    tangent = conv_out[batch:].reshape(probes_here, batch, tile_h, tile_w, chans)
    partial_sum = jnp.sum(signs * tangent, axis=(0, 2, 3, 4))
    velocity = conv_primal + conv_bias
    next_state = (xf + 0.25 * velocity).astype(jnp.bfloat16)
    total = lax.psum(partial_sum, ("gy", "gx", "probe"))
    logp_delta = -0.25 / (probes_here * lax.axis_size("probe")) * total
    return (next_state, logp_delta)


def solution(mesh):

    def body(*args):
        wide = args[6].shape[1] >= 128
        return (travelling_probes if wide else gathered_weights)(*args)

    in_specs = (
        P(None, "gy", "gx", None),
        P("probe", None, "gy", "gx", None),
        P(),
        P(),
        P(),
        P(),
        P(None, "probe", None),
        P(),
    )
    out_specs = (P(None, "gy", "gx", None), P())
    return jax.shard_map(body, mesh=mesh, in_specs=in_specs, out_specs=out_specs, check_vma=False)
```

profile of v0, /device:TPU:0, one launch (start us, length us, event | category | flops | bytes accessed | tf_op | source)
XLA Modules:
  0.0 215.1 jit_solution(14110770725235641444)
XLA Ops:
  7.2 1.2 convert_element_type.24
  8.4 7.9 %all_gather.3 = bf16[4,4,4,4,640]{4,3,2,1,0:T(4,128)(2,1)S(1)} all-gather(bf16[2,4,4,4,640]{4,3,2,1,0:T(4,128)(2,1)S(1)} %convert_element_type.24), channel_id=1, replica_groups=mesh['gy'=4,'gx'=4,'probe'=2] {'probe'}, dimensions={0}, use_global_device_ids=true | all-gather | bytes 491520 | tf_op jit(solution)/shard_map/all_gather | solution.py:45
  16.3 1.1 fusion.56
  17.4 0.7 fusion.66
  18.1 1.3 collective-permute-start.1
  19.4 3.0 %collective-permute-start = (bf16[20,1,4,320]{3,2,1,0:T(4,128)(2,1)}, bf16[20,1,4,320]{3,2,1,0:T(4,128)(2,1)S(1)}, u32[]{:S(2)}, u32[]{:S(2)}) collective-permute-start(bf16[20,1,4,320]{3,2,1,0:T(4,128)(2,1)} %get-tuple-element.21), channel_id=1, source_target_pairs={{0,8},{8,16},{16,24},{1,9},{9,17},{17,25},{2,10},{10,18},{18,26},{... | collective-permute-start | bytes 153608 | tf_op jit(solution)/shard_map/ppermute | solution.py:14
  22.4 0.9 convert_element_type.23
  23.3 1.0 convert_reduce_fusion.1
  24.3 0.8 dynamic-slice.2
  25.5 1.4 concatenate.27
  27.1 1.3 maximum_reduce_fusion
  28.4 61.5 %psum.21 = f32[10,4,32]{2,1,0:T(4,128)S(1)} all-reduce(f32[10,4,32]{2,1,0:T(4,128)S(1)} %maximum_reduce_fusion), channel_id=1, replica_groups=mesh['gy'=4,'gx'=4,'probe'=2] {'gy','gx'}, use_global_device_ids=true, to_apply=%region_5.0 | all-reduce | flops 1280 | bytes 10240 | tf_op jit(solution)/shard_map/psum | solution.py:61
  90.0 1.1 broadcast_in_dim.44
  91.1 1.5 reshape.118
  92.6 0.9 fusion.57
  93.6 0.7 dynamic-slice_add_fusion
  94.3 0.7 broadcast_and_fusion
  94.9 0.7 constant_dynamic-slice_fusion
  96.3 1.3 collective-permute-start.3
  97.6 4.6 %collective-permute-start.2 = (bf16[20,6,1,320]{3,2,1,0:T(2,128)(2,1)S(1)}, bf16[20,6,1,320]{3,2,1,0:T(2,128)(2,1)S(1)}, u32[]{:S(2)}, u32[]{:S(2)}) collective-permute-start(bf16[20,6,1,320]{3,2,1,0:T(2,128)(2,1)S(1)} %get-tuple-element.19), channel_id=1, source_target_pairs={{0,2},{2,4},{4,6},{1,3},{3,5},{5,7},{8,10},{10,12},{12,14},{9,11},... | collective-permute-start | bytes 230408 | tf_op jit(solution)/shard_map/ppermute | solution.py:14
  102.3 1.5 collective-permute-done.3
  103.7 1.5 collective-permute-done.2
  105.2 1.7 select_bitcast_fusion
  106.9 0.8 fusion.50
  107.8 0.9 fusion.67
  108.6 1.4 reshape.119
  110.1 1.4 reshape.120
  111.5 1.4 reshape.121
  113.0 1.4 reshape.122
  114.4 1.4 reshape.123
  115.8 1.4 reshape.124
  117.3 1.4 reshape.125
  118.7 1.5 reshape.126
  120.2 1.4 reshape.127
  121.6 1.3 fusion.21
  122.9 1.2 convolution_add_fusion.15
  124.2 1.2 convolution_add_fusion.14
  125.4 1.2 convolution_add_fusion.13
  126.6 1.2 convolution_add_fusion.12
  127.9 1.2 convolution_add_fusion.11
  129.1 1.2 convolution_add_fusion.10
  130.4 1.2 convolution_add_fusion.9
  131.6 1.9 convolution_add_fusion.8
  133.5 1.6 reshape.128
  135.1 1.5 fusion.2
  136.6 1.2 multiply_convert_fusion
  137.8 1.7 fusion.64
  139.5 0.8 reshape.130
  140.3 1.4 fusion.19
  141.8 1.7 reshape.131
  143.4 1.7 reshape.132
  145.1 1.7 reshape.133
  146.8 1.7 reshape.134
  148.5 1.7 reshape.135
  150.2 1.7 reshape.136
  151.9 1.7 reshape.137
  153.6 1.7 reshape.138
  155.3 1.6 convolution_add_fusion.7
  156.9 1.5 convolution_add_fusion.6
  158.4 1.3 convolution_add_fusion.5
  161.2 1.2 convolution_add_fusion
  162.4 1.3 reshape.139
  164.0 42.0 %psum.23 = f32[4]{0:T(128)S(1)} all-reduce(f32[4]{0:T(128)S(1)} %fusion.1), channel_id=1, replica_groups=mesh['gy'=4,'gx'=4,'probe'=2] {'gy','gx','probe'}, use_global_device_ids=true, to_apply=%region_8.9 | all-reduce | flops 4 | bytes 32 | tf_op jit(solution)/shard_map/psum | solution.py:94
  206.6 1.7 add_convert_fusion
  (59 shorter events, 3.8 us)
Async XLA Ops:
  7.2 85.5 %copy-start = (f32[1000,640]{1,0:T(8,128)S(1)}, f32[1000,640]{1,0:T(8,128)}, u32[]{:S(2)}) copy-start(f32[1000,640]{1,0:T(8,128)} %param.11) | copy-start | bytes 7680004
  7.2 85.5 %copy-start.16 = (s32[4]{0:T(128)S(1)}, s32[4]{0:T(128)}, u32[]{:S(2)}) copy-start(s32[4]{0:T(128)} %param.10) | copy-start | bytes 52
  7.2 199.4 %all-reduce.2.cloned.1.call-start = ((), (), s32[]{:S(2)}) async-start(), calls=%async_computation | async-start | bytes 327680 | tf_op jit(solution)/shard_map/psum | solution.py:89
  17.4 78.3 %copy-start.15 = (f32[640]{0:T(1024)S(1)}, f32[640]{0:T(1024)}, u32[]{:S(2)}) copy-start(f32[640]{0:T(1024)} %param.12) | copy-start | bytes 7684
  18.1 77.7 %collective-permute-start.1 = (bf16[20,1,4,320]{3,2,1,0:T(4,128)(2,1)}, bf16[20,1,4,320]{3,2,1,0:T(4,128)(2,1)S(1)}, u32[]{:S(2)}, u32[]{:S(2)}) collective-permute-start(bf16[20,1,4,320]{3,2,1,0:T(4,128)(2,1)} %get-tuple-element.22), channel_id=1, source_target_pairs={{8,0},{16,8},{24,16},{9,1},{17,9},{25,17},{10,2},{18,10},{26,18},{... | collective-permute-start | bytes 153608 | tf_op jit(solution)/shard_map/ppermute | solution.py:17
  19.4 76.4 %collective-permute-start = (bf16[20,1,4,320]{3,2,1,0:T(4,128)(2,1)}, bf16[20,1,4,320]{3,2,1,0:T(4,128)(2,1)S(1)}, u32[]{:S(2)}, u32[]{:S(2)}) collective-permute-start(bf16[20,1,4,320]{3,2,1,0:T(4,128)(2,1)} %get-tuple-element.21), channel_id=1, source_target_pairs={{0,8},{8,16},{16,24},{1,9},{9,17},{17,25},{2,10},{10,18},{18,26},{... | collective-permute-start | bytes 153608 | tf_op jit(solution)/shard_map/ppermute | solution.py:14
  96.3 7.4 %collective-permute-start.3 = (bf16[20,6,1,320]{3,2,1,0:T(2,128)(2,1)S(1)}, bf16[20,6,1,320]{3,2,1,0:T(2,128)(2,1)S(1)}, u32[]{:S(2)}, u32[]{:S(2)}) collective-permute-start(bf16[20,6,1,320]{3,2,1,0:T(2,128)(2,1)S(1)} %get-tuple-element.20), channel_id=1, source_target_pairs={{2,0},{4,2},{6,4},{3,1},{5,3},{7,5},{10,8},{12,10},{14,12},{11,9},... | collective-permute-start | bytes 230408 | tf_op jit(solution)/shard_map/ppermute | solution.py:17
  97.6 7.6 %collective-permute-start.2 = (bf16[20,6,1,320]{3,2,1,0:T(2,128)(2,1)S(1)}, bf16[20,6,1,320]{3,2,1,0:T(2,128)(2,1)S(1)}, u32[]{:S(2)}, u32[]{:S(2)}) collective-permute-start(bf16[20,6,1,320]{3,2,1,0:T(2,128)(2,1)S(1)} %get-tuple-element.19), channel_id=1, source_target_pairs={{0,2},{2,4},{4,6},{1,3},{3,5},{5,7},{8,10},{10,12},{12,14},{9,11},... | collective-permute-start | bytes 230408 | tf_op jit(solution)/shard_map/ppermute | solution.py:14
  102.2 4.7 %copy-start.13 = (f32[4,320]{1,0:T(4,128)}, f32[4,320]{1,0:T(4,128)S(1)}, u32[]{:S(2)}) copy-start(f32[4,320]{1,0:T(4,128)S(1)} %get-tuple-element.35) | copy-start | bytes 15364
  103.7 3.2 %copy-start.7 = (bf16[20,6,1,320]{3,2,1,0:T(2,128)(2,1)}, bf16[20,6,1,320]{3,2,1,0:T(2,128)(2,1)S(1)}, u32[]{:S(2)}) copy-start(bf16[20,6,1,320]{3,2,1,0:T(2,128)(2,1)S(1)} %collective-permute-done.3) | copy-start | bytes 230404
  105.2 2.5 %copy-start.8 = (bf16[20,6,1,320]{3,2,1,0:T(2,128)(2,1)}, bf16[20,6,1,320]{3,2,1,0:T(2,128)(2,1)S(1)}, u32[]{:S(2)}) copy-start(bf16[20,6,1,320]{3,2,1,0:T(2,128)(2,1)S(1)} %collective-permute-done.2) | copy-start | bytes 230404
  121.6 6.3 %copy-start.12 = (bf16[64,320]{1,0:T(8,128)(2,1)S(1)}, bf16[64,320]{1,0:T(8,128)(2,1)}, u32[]{:S(2)}) copy-start(bf16[64,320]{1,0:T(8,128)(2,1)} %reshape.124) | copy-start | bytes 122884
  121.6 7.5 %copy-start.11 = (bf16[64,320]{1,0:T(8,128)(2,1)S(1)}, bf16[64,320]{1,0:T(8,128)(2,1)}, u32[]{:S(2)}) copy-start(bf16[64,320]{1,0:T(8,128)(2,1)} %reshape.125) | copy-start | bytes 122884
  121.6 8.7 %copy-start.9 = (bf16[64,320]{1,0:T(8,128)(2,1)S(1)}, bf16[64,320]{1,0:T(8,128)(2,1)}, u32[]{:S(2)}) copy-start(bf16[64,320]{1,0:T(8,128)(2,1)} %reshape.126) | copy-start | bytes 122884
  121.6 9.9 %copy-start.10 = (bf16[64,320]{1,0:T(8,128)(2,1)S(1)}, bf16[64,320]{1,0:T(8,128)(2,1)}, u32[]{:S(2)}) copy-start(bf16[64,320]{1,0:T(8,128)(2,1)} %reshape.127) | copy-start | bytes 122884
  155.3 3.1 %copy-start.1 = (bf16[9,320,640]{2,1,0:T(8,128)(2,1)S(1)}, bf16[9,320,640]{2,1,0:T(8,128)(2,1)}, u32[]{:S(2)}) copy-start(bf16[9,320,640]{2,1,0:T(8,128)(2,1)} %param.14) | copy-start | bytes 11059204
  155.3 4.5 %copy-start.6 = (bf16[256,320]{1,0:T(8,128)(2,1)S(1)}, bf16[256,320]{1,0:T(8,128)(2,1)}, u32[]{:S(2)}) copy-start(bf16[256,320]{1,0:T(8,128)(2,1)} %reshape.134) | copy-start | bytes 491524
  155.3 4.8 %copy-start.5 = (bf16[256,320]{1,0:T(8,128)(2,1)S(1)}, bf16[256,320]{1,0:T(8,128)(2,1)}, u32[]{:S(2)}) copy-start(bf16[256,320]{1,0:T(8,128)(2,1)} %reshape.135) | copy-start | bytes 491524
  156.9 3.6 %copy-start.4 = (bf16[256,320]{1,0:T(8,128)(2,1)S(1)}, bf16[256,320]{1,0:T(8,128)(2,1)}, u32[]{:S(2)}) copy-start(bf16[256,320]{1,0:T(8,128)(2,1)} %reshape.136) | copy-start | bytes 491524
  158.4 2.5 %copy-start.2 = (bf16[256,320]{1,0:T(8,128)(2,1)S(1)}, bf16[256,320]{1,0:T(8,128)(2,1)}, u32[]{:S(2)}) copy-start(bf16[256,320]{1,0:T(8,128)(2,1)} %reshape.137) | copy-start | bytes 491524
  159.7 1.5 copy-start.3
  160.5 46.1 %copy-start.14 = (f32[640]{0:T(1024)S(1)}, f32[640]{0:T(1024)}, u32[]{:S(2)}) copy-start(f32[640]{0:T(1024)} %param.15) | copy-start | bytes 7684
Sparse Core Ops, SparseCore 0:
  164.2 23.1 all-reduce.1
where the time goes:
time: 217 us; the launch traced here: 215 us
  blocking collectives  111 us (51%)
  local copies, waits for them, and re-layouts  39.6 us (18%)
  matrix products  21.1 us (10%)
  other arithmetic  15.3 us (7%)
  between operations  14.5 us (7%)
  starting transfers between devices  10.2 us (5%)
  waiting for transfers between devices  2.96 us (1%)
    psum x1, blocking collectives, travelling_probes(): sums = lax.psum(sums, ('gy', 'gx')) / count  61.5 us
    psum x1, blocking collectives, travelling_probes(): lax.psum(jnp.sum(signs_f * tangent, axis=(0, 2, 3, 4)), ('gy', 'gx', 'pro...  42 us
    reshape x18, local copies, waits for them, and re-layouts, local_conv(): padded[:, row_off:row_off + height, col_off:col_off + width, :]  27.3 us
    dot_general x18, matrix products, local_conv(): jnp.dot(window, weight[tap], preferred_element_type=jnp.float32)  20.2 us
    all_gather x1, blocking collectives, travelling_probes(): lax.all_gather(probe_signs.astype(jnp.bfloat16), 'probe', axis=0, tiled=T...  7.85 us
    ppermute x2, starting transfers between devices, with_halo(): lax.ppermute(lax.slice_in_dim(block, block.shape[dim] - width, None, axis...  7.59 us
  transfers between devices with their start and end apart: 5, of which 2 were waited for; matrix products, arithmetic and copies ran while one was open for 6% of the time, Pallas kernels for 0%

commit v1 on v0

--- a/solution.py
+++ b/solution.py
@@ -58,7 +58,7 @@
     cells_u = jnp.stack([jnp.sum(signs_f, axis=(2, 3)), jnp.sum(signs_f * xf[None], axis=(2, 3))])
     cells = jnp.concatenate([cells_x, cells_u.reshape(2 * probes, batch, chans)], axis=0)
     sums = jnp.sum(cells.reshape(2 + 2 * probes, batch, GROUPS, group_width), axis=3)
-    sums = lax.psum(sums, ("gy", "gx")) / count
+    sums = jnp.sum(lax.all_gather(sums, ("gy", "gx")), axis=0) / count
     mean_x, mean_xx = (sums[0], sums[1])
     mean_u, cross = (sums[2 : 2 + probes], sums[2 + probes :])
     sigma = jnp.sqrt(mean_xx - mean_x * mean_x + 1e-05)

time: 217 us -> 191 us (0.88)
  blocking collectives: 111 us -> 84.6 us
    psum x1 -> x0, blocking collectives: 61.5 us -> none  [travelling_probes(): sums = lax.psum(sums, ('gy', 'gx')) / count]
    all_gather x0 -> x1, blocking collectives: none -> 34.6 us  [travelling_probes(): sums = jnp.sum(lax.all_gather(sums, ('gy', 'gx')), axis=0) / count]
where the time goes in v1:
time: 191 us; the launch traced here: 189 us
  blocking collectives  84.6 us (44%)
  local copies, waits for them, and re-layouts  39.6 us (21%)
  matrix products  21.2 us (11%)
  other arithmetic  15.6 us (8%)
  between operations  14.4 us (8%)
  starting transfers between devices  10.8 us (6%)
  waiting for transfers between devices  2.96 us (2%)
    psum x1, blocking collectives, travelling_probes(): lax.psum(jnp.sum(signs_f * tangent, axis=(0, 2, 3, 4)), ('gy', 'gx', 'pro...  42.1 us
    all_gather x1, blocking collectives, travelling_probes(): sums = jnp.sum(lax.all_gather(sums, ('gy', 'gx')), axis=0) / count  34.6 us
    reshape x18, local copies, waits for them, and re-layouts, local_conv(): padded[:, row_off:row_off + height, col_off:col_off + width, :]  27.3 us
    dot_general x18, matrix products, local_conv(): jnp.dot(window, weight[tap], preferred_element_type=jnp.float32)  20.2 us
    ppermute x2, starting transfers between devices, with_halo(): lax.ppermute(lax.slice_in_dim(block, block.shape[dim] - width, None, axis...  8.22 us
    all_gather x1, blocking collectives, travelling_probes(): lax.all_gather(probe_signs.astype(jnp.bfloat16), 'probe', axis=0, tiled=T...  7.85 us
  transfers between devices with their start and end apart: 5, of which 2 were waited for; matrix products, arithmetic and copies ran while one was open for 6% of the time, Pallas kernels for 0%

profile of v1, /device:TPU:0, one launch (start us, length us, event | category | flops | bytes accessed | tf_op | source)
XLA Modules:
  0.0 189.2 jit_solution(17003219712620143055)
XLA Ops:
  7.2 1.2 convert_element_type.24
  8.4 7.9 %all_gather.9 = bf16[4,4,4,4,640]{4,3,2,1,0:T(4,128)(2,1)S(1)} all-gather(bf16[2,4,4,4,640]{4,3,2,1,0:T(4,128)(2,1)S(1)} %convert_element_type.24), channel_id=1, replica_groups=mesh['gy'=4,'gx'=4,'probe'=2] {'probe'}, dimensions={0}, use_global_device_ids=true | all-gather | bytes 491520 | tf_op jit(solution)/shard_map/all_gather | solution.py:45
  16.3 1.1 fusion.56
  17.4 0.7 fusion.66
  18.1 1.3 collective-permute-start.1
  19.4 3.7 %collective-permute-start = (bf16[20,1,4,320]{3,2,1,0:T(4,128)(2,1)}, bf16[20,1,4,320]{3,2,1,0:T(4,128)(2,1)}, u32[]{:S(2)}, u32[]{:S(2)}) collective-permute-start(bf16[20,1,4,320]{3,2,1,0:T(4,128)(2,1)} %get-tuple-element.21), channel_id=1, source_target_pairs={{0,8},{8,16},{16,24},{1,9},{9,17},{17,25},{2,10},{10,18},{18,26},{... | collective-permute-start | bytes 153608 | tf_op jit(solution)/shard_map/ppermute | solution.py:14
  23.0 0.9 convert_element_type.23
  23.9 1.0 convert_reduce_fusion.1
  24.9 0.8 dynamic-slice.2
  26.1 1.4 concatenate.27
  27.8 1.3 maximum_reduce_fusion
  29.1 34.6 %all-gather = f32[160,4,32]{2,1,0:T(4,128)S(1)} all-gather(f32[10,4,32]{2,1,0:T(4,128)S(1)} %maximum_reduce_fusion), channel_id=2, replica_groups=mesh['gy'=4,'gx'=4,'probe'=2] {'gy','gx'}, dimensions={0}, use_global_device_ids=true | all-gather | bytes 87040 | tf_op jit(solution)/shard_map/all_gather | solution.py:61
  63.9 1.1 broadcast_in_dim.44
  64.9 1.5 reshape.118
  66.5 0.9 fusion.57
  67.5 0.7 broadcast_and_fusion
  68.3 0.7 dynamic_slice.14
  69.0 1.1 pad_maximum_fusion.4
  70.3 1.3 collective-permute-start.3
  71.6 4.6 %collective-permute-start.2 = (bf16[20,6,1,320]{3,2,1,0:T(2,128)(2,1)S(1)}, bf16[20,6,1,320]{3,2,1,0:T(2,128)(2,1)S(1)}, u32[]{:S(2)}, u32[]{:S(2)}) collective-permute-start(bf16[20,6,1,320]{3,2,1,0:T(2,128)(2,1)S(1)} %get-tuple-element.19), channel_id=1, source_target_pairs={{0,2},{2,4},{4,6},{1,3},{3,5},{5,7},{8,10},{10,12},{12,14},{9,11},... | collective-permute-start | bytes 230408 | tf_op jit(solution)/shard_map/ppermute | solution.py:14
  76.3 1.5 collective-permute-done.3
  77.8 1.5 collective-permute-done.2
  79.2 1.7 select_bitcast_fusion
  81.0 0.8 fusion.50
  81.8 0.8 fusion.67
  82.7 1.4 reshape.119
  84.1 1.4 reshape.120
  85.6 1.4 reshape.121
  87.0 1.4 reshape.122
  88.5 1.4 reshape.123
  89.9 1.4 reshape.124
  91.3 1.4 reshape.125
  92.8 1.4 reshape.126
  94.2 1.4 reshape.127
  95.7 1.3 fusion.21
  96.9 1.2 convolution_add_fusion.15
  98.2 1.2 convolution_add_fusion.14
  99.4 1.2 convolution_add_fusion.13
  100.7 1.2 convolution_add_fusion.12
  101.9 1.2 convolution_add_fusion.11
  103.2 1.2 convolution_add_fusion.10
  104.4 1.2 convolution_add_fusion.9
  105.6 1.9 convolution_add_fusion.8
  107.5 1.6 reshape.128
  109.1 1.5 fusion.2
  110.6 1.2 multiply_convert_fusion
  111.8 1.7 fusion.64
  113.5 0.8 reshape.130
  114.3 1.4 fusion.19
  115.7 1.7 reshape.131
  117.4 1.7 reshape.132
  119.1 1.7 reshape.133
  120.8 1.7 reshape.134
  122.5 1.7 reshape.135
  124.2 1.7 reshape.136
  125.9 1.7 reshape.137
  127.6 1.7 reshape.138
  129.3 1.6 convolution_add_fusion.7
  130.9 1.5 convolution_add_fusion.6
  132.4 1.3 convolution_add_fusion.5
  135.2 1.2 convolution_add_fusion
  136.4 1.3 reshape.139
  138.1 42.1 %psum.15 = f32[4]{0:T(128)S(1)} all-reduce(f32[4]{0:T(128)S(1)} %fusion.1), channel_id=1, replica_groups=mesh['gy'=4,'gx'=4,'probe'=2] {'gy','gx','probe'}, use_global_device_ids=true, to_apply=%region_8.9 | all-reduce | flops 4 | bytes 32 | tf_op jit(solution)/shard_map/psum | solution.py:94
  180.7 1.7 add_convert_fusion
  (58 shorter events, 3.7 us)
Async XLA Ops:
  7.2 59.3 %copy-start = (f32[1000,640]{1,0:T(8,128)S(1)}, f32[1000,640]{1,0:T(8,128)}, u32[]{:S(2)}) copy-start(f32[1000,640]{1,0:T(8,128)} %param.11) | copy-start | bytes 7680004
  7.2 59.3 %copy-start.15 = (s32[4]{0:T(128)S(1)}, s32[4]{0:T(128)}, u32[]{:S(2)}) copy-start(s32[4]{0:T(128)} %param.10) | copy-start | bytes 52
  7.2 173.5 %all-reduce.2.cloned.1.call-start = ((), (), s32[]{:S(2)}) async-start(), calls=%async_computation | async-start | bytes 327680 | tf_op jit(solution)/shard_map/psum | solution.py:89
  18.1 50.9 %collective-permute-start.1 = (bf16[20,1,4,320]{3,2,1,0:T(4,128)(2,1)}, bf16[20,1,4,320]{3,2,1,0:T(4,128)(2,1)S(1)}, u32[]{:S(2)}, u32[]{:S(2)}) collective-permute-start(bf16[20,1,4,320]{3,2,1,0:T(4,128)(2,1)} %get-tuple-element.22), channel_id=1, source_target_pairs={{8,0},{16,8},{24,16},{9,1},{17,9},{25,17},{10,2},{18,10},{26,18},{... | collective-permute-start | bytes 153608 | tf_op jit(solution)/shard_map/ppermute | solution.py:17
  19.4 49.6 %collective-permute-start = (bf16[20,1,4,320]{3,2,1,0:T(4,128)(2,1)}, bf16[20,1,4,320]{3,2,1,0:T(4,128)(2,1)}, u32[]{:S(2)}, u32[]{:S(2)}) collective-permute-start(bf16[20,1,4,320]{3,2,1,0:T(4,128)(2,1)} %get-tuple-element.21), channel_id=1, source_target_pairs={{0,8},{8,16},{16,24},{1,9},{9,17},{17,25},{2,10},{10,18},{18,26},{... | collective-permute-start | bytes 153608 | tf_op jit(solution)/shard_map/ppermute | solution.py:14
  23.9 44.3 %copy-start.14 = (f32[640]{0:T(1024)S(1)}, f32[640]{0:T(1024)}, u32[]{:S(2)}) copy-start(f32[640]{0:T(1024)} %param.12) | copy-start | bytes 7684
  70.3 7.4 %collective-permute-start.3 = (bf16[20,6,1,320]{3,2,1,0:T(2,128)(2,1)S(1)}, bf16[20,6,1,320]{3,2,1,0:T(2,128)(2,1)S(1)}, u32[]{:S(2)}, u32[]{:S(2)}) collective-permute-start(bf16[20,6,1,320]{3,2,1,0:T(2,128)(2,1)S(1)} %get-tuple-element.20), channel_id=1, source_target_pairs={{2,0},{4,2},{6,4},{3,1},{5,3},{7,5},{10,8},{12,10},{14,12},{11,9},... | collective-permute-start | bytes 230408 | tf_op jit(solution)/shard_map/ppermute | solution.py:17
  71.6 7.6 %collective-permute-start.2 = (bf16[20,6,1,320]{3,2,1,0:T(2,128)(2,1)S(1)}, bf16[20,6,1,320]{3,2,1,0:T(2,128)(2,1)S(1)}, u32[]{:S(2)}, u32[]{:S(2)}) collective-permute-start(bf16[20,6,1,320]{3,2,1,0:T(2,128)(2,1)S(1)} %get-tuple-element.19), channel_id=1, source_target_pairs={{0,2},{2,4},{4,6},{1,3},{3,5},{5,7},{8,10},{10,12},{12,14},{9,11},... | collective-permute-start | bytes 230408 | tf_op jit(solution)/shard_map/ppermute | solution.py:14
  77.8 3.2 %copy-start.7 = (bf16[20,6,1,320]{3,2,1,0:T(2,128)(2,1)}, bf16[20,6,1,320]{3,2,1,0:T(2,128)(2,1)S(1)}, u32[]{:S(2)}) copy-start(bf16[20,6,1,320]{3,2,1,0:T(2,128)(2,1)S(1)} %collective-permute-done.3) | copy-start | bytes 230404
  79.2 2.6 %copy-start.8 = (bf16[20,6,1,320]{3,2,1,0:T(2,128)(2,1)}, bf16[20,6,1,320]{3,2,1,0:T(2,128)(2,1)S(1)}, u32[]{:S(2)}) copy-start(bf16[20,6,1,320]{3,2,1,0:T(2,128)(2,1)S(1)} %collective-permute-done.2) | copy-start | bytes 230404
  95.7 6.3 %copy-start.12 = (bf16[64,320]{1,0:T(8,128)(2,1)S(1)}, bf16[64,320]{1,0:T(8,128)(2,1)}, u32[]{:S(2)}) copy-start(bf16[64,320]{1,0:T(8,128)(2,1)} %reshape.124) | copy-start | bytes 122884
  95.7 7.5 %copy-start.11 = (bf16[64,320]{1,0:T(8,128)(2,1)S(1)}, bf16[64,320]{1,0:T(8,128)(2,1)}, u32[]{:S(2)}) copy-start(bf16[64,320]{1,0:T(8,128)(2,1)} %reshape.125) | copy-start | bytes 122884
  95.7 8.7 %copy-start.9 = (bf16[64,320]{1,0:T(8,128)(2,1)S(1)}, bf16[64,320]{1,0:T(8,128)(2,1)}, u32[]{:S(2)}) copy-start(bf16[64,320]{1,0:T(8,128)(2,1)} %reshape.126) | copy-start | bytes 122884
  95.7 9.9 %copy-start.10 = (bf16[64,320]{1,0:T(8,128)(2,1)S(1)}, bf16[64,320]{1,0:T(8,128)(2,1)}, u32[]{:S(2)}) copy-start(bf16[64,320]{1,0:T(8,128)(2,1)} %reshape.127) | copy-start | bytes 122884
  129.3 3.1 %copy-start.1 = (bf16[9,320,640]{2,1,0:T(8,128)(2,1)S(1)}, bf16[9,320,640]{2,1,0:T(8,128)(2,1)}, u32[]{:S(2)}) copy-start(bf16[9,320,640]{2,1,0:T(8,128)(2,1)} %param.14) | copy-start | bytes 11059204
  129.3 4.5 %copy-start.6 = (bf16[256,320]{1,0:T(8,128)(2,1)S(1)}, bf16[256,320]{1,0:T(8,128)(2,1)}, u32[]{:S(2)}) copy-start(bf16[256,320]{1,0:T(8,128)(2,1)} %reshape.134) | copy-start | bytes 491524
  129.3 4.8 %copy-start.5 = (bf16[256,320]{1,0:T(8,128)(2,1)S(1)}, bf16[256,320]{1,0:T(8,128)(2,1)}, u32[]{:S(2)}) copy-start(bf16[256,320]{1,0:T(8,128)(2,1)} %reshape.135) | copy-start | bytes 491524
  130.9 3.6 %copy-start.4 = (bf16[256,320]{1,0:T(8,128)(2,1)S(1)}, bf16[256,320]{1,0:T(8,128)(2,1)}, u32[]{:S(2)}) copy-start(bf16[256,320]{1,0:T(8,128)(2,1)} %reshape.136) | copy-start | bytes 491524
  132.4 2.5 %copy-start.2 = (bf16[256,320]{1,0:T(8,128)(2,1)S(1)}, bf16[256,320]{1,0:T(8,128)(2,1)}, u32[]{:S(2)}) copy-start(bf16[256,320]{1,0:T(8,128)(2,1)} %reshape.137) | copy-start | bytes 491524
  133.7 1.5 copy-start.3
  134.5 46.2 %copy-start.13 = (f32[640]{0:T(1024)S(1)}, f32[640]{0:T(1024)}, u32[]{:S(2)}) copy-start(f32[640]{0:T(1024)} %param.15) | copy-start | bytes 7684
Sparse Core Ops, SparseCore 0:
  138.2 23.2 all-reduce.1
